TPU v7x, 32 devices: a whole 2x2x4 slice. The times are simulated.
32 devices in a mesh: occ: 16 (over z, y, core), vir: 2 (over x).
Axes of the slice: x: 2, y: 2, z: 4, core: 2. Of those that a mesh axis runs over, the one named last changes fastest.
Arguments:
- lambda_triples: bfloat16 [256, 320, 320], P('occ', 'vir'), may hold values from -6 to 6
- amplitude_triples: bfloat16 [256, 320, 320], P('occ', 'vir'), may hold values from -6 to 6
- spin_extent: int32 [256], P('occ'), may hold values from 80 to 320
- ladder_weight: bfloat16 [320, 320], P(None, 'vir'), may hold values from -0.3125 to 0.3125
- cycle_weight: bfloat16 [320, 40], replicated, may hold values from -0.3125 to 0.3125
- lambda_doubles: bfloat16 [40, 320], P(None, 'vir'), may hold values from -1 to 1
Outputs:
- residual: bfloat16 [256, 320, 320], P('occ', 'vir')
All inputs are finite; a program needn't handle non-finite values.
Results may differ from a plain program's by a relative error of at most 0.0043.
Values may be sent and summed in bfloat16 or wider, within the bound.
No kernel may reach another device: no remote copies, remote signals or barrier semaphores. Data moves between devices by JAX's collectives and lax.ppermute only.
A program may use at most 64 MiB of HBM per device.

v0:
```python
import jax
import jax.numpy as jnp
from jax import lax
from jax.sharding import PartitionSpec as P


def on_device(
    lambda_triples, amplitude_triples, spin_extent, ladder_weight, cycle_weight, lambda_doubles
):
    f32 = jnp.float32
    width = lambda_triples.shape[2]
    triples_all = lambda_triples.shape[0] * lax.axis_size("occ")
    columns = jnp.arange(width, dtype=jnp.int32)
    keep = columns[None, :] < spin_extent[:, None]
    masked = jnp.where(keep[:, None, :], lambda_triples, jnp.zeros_like(lambda_triples))
    ladder_full, doubles_full = (
        lax.all_gather(ladder_weight, "vir", axis=1, tiled=True),
        lax.all_gather(lambda_doubles, "vir", axis=1, tiled=True),
    )
    ladder_term = jnp.einsum("tae,eb->tab", masked, ladder_full, preferred_element_type=f32)
    cycle_mid = jnp.einsum(
        "tae,em->tam", amplitude_triples, cycle_weight, preferred_element_type=f32
    ).astype(jnp.bfloat16)
    cycle_term = jnp.einsum("tam,mb->tab", cycle_mid, doubles_full, preferred_element_type=f32)
    partial_density = jnp.einsum(
        "tae,tbe->ab",
        masked,
        lax.all_gather(amplitude_triples, "vir", axis=1, tiled=True),
        preferred_element_type=f32,
    )
    density = lax.psum(partial_density, "occ")
    density = (density / jnp.sqrt(f32(triples_all * width))).astype(jnp.bfloat16)
    density_term = jnp.einsum(
        "ac,tcb->tab",
        density,
        lax.all_gather(masked, "vir", axis=1, tiled=True),
        preferred_element_type=f32,
    )
    density_term = density_term / jnp.sqrt(f32(width))
    return (ladder_term + cycle_term + density_term).astype(jnp.bfloat16)


def solution(mesh):
    return jax.shard_map(
        on_device,
        mesh=mesh,
        in_specs=(
            P("occ", "vir", None),
            P("occ", "vir", None),
            P("occ"),
            P(None, "vir"),
            P(),
            P(None, "vir"),
        ),
        out_specs=P("occ", "vir", None),
        check_vma=False,
    )
```

profile of v0, /device:TPU:8, one launch (start us, length us, event | category | flops | bytes accessed | tf_op | source)
XLA Modules:
  0.0 227.4 jit_solution(11360172198900712387)
XLA Ops:
  6.5 0.0 copy-start
  6.5 0.0 copy-start.3
  6.5 0.0 copy-start.2
  6.5 0.0 all-gather.6.cloned.1.call-start
  6.5 0.7 all-gather.6.cloned.1.call-update
  7.3 0.0 all-gather.4.cloned.1.call-start
  7.3 0.7 iota_compare_fusion
  8.0 3.0 %broadcast_select_fusion = bf16[16,160,320]{2,1,0:T(8,128)(2,1)} fusion(bf16[16,160,320]{2,1,0:T(8,128)(2,1)} %param.6, pred[16,320]{1,0:T(8,128)(4,1)S(1)} %iota_compare_fusion), kind=kLoop, calls=%fused_computation.2 | loop fusion | flops 819200 | bytes 3281920 | tf_op jit(solution)/shard_map/jit(_where)/select_n | solution.py:15
  11.1 0.0 copy-start.1
  11.1 0.0 all-gather.4.cloned.1.call-update
  11.1 0.0 all-reduce.2.cloned.1.call-start
  11.2 0.0 copy-done.3
  11.2 4.6 %all-gather = bf16[2,160,40]{1,2,0:T(8,128)(2,1)S(1)} all-gather(bf16[1,160,40]{1,2,0:T(8,128)(2,1)S(1)} %bitcast.27), channel_id=1, replica_groups=mesh['occ'=16,'vir'=2] {'vir'}, dimensions={0}, use_global_device_ids=true | all-gather | bytes 38400 | tf_op jit(solution)/shard_map/all_gather | solution.py:18
  15.8 0.1 reshape.21
  15.9 0.0 copy-done.2
  15.9 6.4 %all_gather.12 = bf16[320,320]{0,1:T(8,128)(2,1)S(1)} all-gather(bf16[320,160]{0,1:T(8,128)(2,1)S(1)} %copy-done.2), channel_id=1, replica_groups=mesh['occ'=16,'vir'=2] {'vir'}, dimensions={1}, use_global_device_ids=true | all-gather | bytes 307200 | tf_op jit(solution)/shard_map/all_gather | solution.py:17
  22.3 4.9 %fusion.2 = f32[16,160,320]{2,1,0:T(8,128)} fusion(bf16[16,160,320]{2,1,0:T(8,128)(2,1)} %broadcast_select_fusion, bf16[320,320]{0,1:T(8,128)(2,1)S(1)} %all_gather.12), kind=kOutput, calls=%fused_computation.6 | convolution fusion | flops 524288000 | bytes 5120000 | tf_op jit(solution)/shard_map/tae,eb->tab/dot_general | solution.py:20
  27.2 36.7 %all-gather.6.cloned.1.call-done = bf16[16,320,320]{2,1,0:T(8,128)(2,1)} async-done(((bf16[16,160,320]{2,1,0:T(8,128)(2,1)}), bf16[16,320,320]{2,1,0:T(8,128)(2,1)}) %all-gather.6.cloned.1.call-update) | async-done | bytes 3276816 | tf_op jit(solution)/shard_map/all_gather | solution.py:28
  63.9 0.0 copy-done.1
  63.9 4.4 %convolution_bitcast_fusion = f32[160,320]{1,0:T(8,128)} fusion(bf16[16,160,320]{2,1,0:T(8,128)(2,1)S(1)} %copy-done.1, bf16[16,320,320]{2,1,0:T(8,128)(2,1)} %all-gather.6.cloned.1.call-done), kind=kOutput, calls=%fused_computation.5 | convolution fusion | flops 524288000 | bytes 5120000 | tf_op jit(solution)/shard_map/tae,tbe->ab/dot_general | solution.py:25
  68.3 0.0 all-reduce.2.cloned.1.call-update
  68.3 0.0 copy-done
  68.3 5.2 %fusion.1 = f32[16,160,320]{2,1,0:T(8,128)} fusion(bf16[320,40,1]{0,1,2:T(8,128)(2,1)S(1)} %reshape.21, bf16[16,160,320]{2,1,0:T(8,128)(2,1)} %param.7, bf16[320,40]{0,1:T(8,128)(2,1)S(1)} %copy-done), kind=kOutput, calls=%fused_computation.4 | convolution fusion | flops 131174400 | bytes 4966400 | tf_op jit(solution)/shard_map/tam,mb->tab/dot_general | solution.py:24
  73.5 46.9 %all-gather.4.cloned.1.call-done = bf16[16,320,320]{2,1,0:T(8,128)(2,1)} async-done(((bf16[16,160,320]{2,1,0:T(8,128)(2,1)}), bf16[16,320,320]{2,1,0:T(8,128)(2,1)}) %all-gather.4.cloned.1.call-update) | async-done | bytes 3276816 | tf_op jit(solution)/shard_map/all_gather | solution.py:36
  120.4 93.5 %all-reduce.2.cloned.1.call-done = f32[160,320]{1,0:T(8,128)} async-done(((f32[160,320]{1,0:T(8,128)}), f32[160,320]{1,0:T(8,128)}) %all-reduce.2.cloned.1.call-update) | async-done | bytes 204816 | tf_op jit(solution)/shard_map/psum | solution.py:31
  213.9 7.0 %fusion = bf16[16,160,320]{2,1,0:T(8,128)(2,1)} fusion(f32[16,160,320]{2,1,0:T(8,128)} %fusion.2, f32[16,160,320]{2,1,0:T(8,128)} %fusion.1, bf16[16,320,320]{2,1,0:T(8,128)(2,1)} %all-gather.4.cloned.1.call-done, f32[160,320]{1,0:T(8,128)} %all-reduce.2.cloned.1.call-done), kind=kOutput, calls=%fused_computation.1 | convolution fusion | flops 527667200 | bytes 11673600 | tf_op jit(solution)/shard_map/ac,tcb->tab/dot_general | solution.py:33
  (1 shorter events, 0.0 us)
Async XLA Ops:
  6.5 61.8 %copy-start = (bf16[320,40]{0,1:T(8,128)(2,1)S(1)}, bf16[320,40]{0,1:T(8,128)(2,1)}, u32[]{:S(2)}) copy-start(bf16[320,40]{0,1:T(8,128)(2,1)} %param.10) | copy-start | bytes 76804
  6.5 4.6 %copy-start.3 = (bf16[40,160]{1,0:T(8,128)(2,1)S(1)}, bf16[40,160]{1,0:T(8,128)(2,1)}, u32[]{:S(2)}) copy-start(bf16[40,160]{1,0:T(8,128)(2,1)} %param.11) | copy-start | bytes 38404
  6.5 9.4 %copy-start.2 = (bf16[320,160]{0,1:T(8,128)(2,1)S(1)}, bf16[320,160]{0,1:T(8,128)(2,1)}, u32[]{:S(2)}) copy-start(bf16[320,160]{0,1:T(8,128)(2,1)} %param.9) | copy-start | bytes 307204
  6.5 57.4 %all-gather.6.cloned.1.call-start = ((), (), s32[]{:S(2)}) async-start(), calls=%async_computation.1 | async-start | bytes 5898240 | tf_op jit(solution)/shard_map/all_gather | solution.py:28
  7.3 113.1 %all-gather.4.cloned.1.call-start = ((), (), s32[]{:S(2)}) async-start(), calls=%async_computation | async-start | bytes 5898240 | tf_op jit(solution)/shard_map/all_gather | solution.py:36
  11.1 52.8 %copy-start.1 = (bf16[16,160,320]{2,1,0:T(8,128)(2,1)S(1)}, bf16[16,160,320]{2,1,0:T(8,128)(2,1)}, u32[]{:S(2)}) copy-start(bf16[16,160,320]{2,1,0:T(8,128)(2,1)} %broadcast_select_fusion) | copy-start | bytes 4915204
  11.1 202.8 %all-reduce.2.cloned.1.call-start = ((), (), s32[]{:S(2)}) async-start(), calls=%async_computation.2 | async-start | bytes 491520 | tf_op jit(solution)/shard_map/psum | solution.py:31
Sparse Core Ops, SparseCore 0:
  8.9 54.9 all-gather.5
  65.4 54.8 all-gather.3
  123.8 90.0 all-reduce.1
where the time goes:
time: 228 us; the launch traced here: 227 us
  waiting for transfers between devices  178 us (78%)
  matrix products  21.4 us (9%)
  between operations  13.1 us (6%)
  blocking collectives  11 us (5%)
  other arithmetic  3.77 us (2%)
    psum x1, waiting for transfers between devices, on_device(): density = lax.psum(partial_density, 'occ')  93.5 us
    all_gather x1, waiting for transfers between devices, on_device(): lax.all_gather(masked, 'vir', axis=1, tiled=True)  46.9 us
    all_gather x1, waiting for transfers between devices, on_device(): lax.all_gather(amplitude_triples, 'vir', axis=1, tiled=True)  36.7 us
    dot_general x1, matrix products, on_device(): jnp.einsum('ac,tcb->tab', density, lax.all_gather(masked, 'vir', axis=1,...  6.97 us
    all_gather x1, blocking collectives, on_device(): lax.all_gather(ladder_weight, 'vir', axis=1, tiled=True)  6.43 us
    dot_general x1, matrix products, on_device(): jnp.einsum('tam,mb->tab', cycle_mid, doubles_full, preferred_element_type...  5.16 us
    dot_general x1, matrix products, on_device(): jnp.einsum('tae,eb->tab', masked, ladder_full, preferred_element_type=f32)  4.91 us
    all_gather x1, blocking collectives, on_device(): lax.all_gather(lambda_doubles, 'vir', axis=1, tiled=True)  4.59 us
  transfers between devices with their start and end apart: 3, of which 3 were waited for; matrix products, arithmetic and copies ran while one was open for 8% of the time, Pallas kernels for 0%

commit v1 on v0

--- a/solution.py
+++ b/solution.py
@@ -2,6 +2,12 @@
 import jax.numpy as jnp
 from jax import lax
 from jax.sharding import PartitionSpec as P
+
+
+def point_scenes_in(field_in, dim_k):
+    moved = list(field_in.shape[1:])
+    moved[dim_k] *= field_in.shape[0]
+    return jnp.moveaxis(field_in, 0, dim_k).reshape(moved)
 
 
 def on_device(
@@ -22,11 +28,29 @@
         "tae,em->tam", amplitude_triples, cycle_weight, preferred_element_type=f32
     ).astype(jnp.bfloat16)
     cycle_term = jnp.einsum("tam,mb->tab", cycle_mid, doubles_full, preferred_element_type=f32)
-    partial_density = jnp.einsum(
-        "tae,tbe->ab",
-        masked,
-        lax.all_gather(amplitude_triples, "vir", axis=1, tiled=True),
-        preferred_element_type=f32,
+
+    def show_paths_in(sample, which_axis, along_dim, slab_in, array_axis):
+        later = lax.axis_size(which_axis)
+        aux = lax.axis_index(which_axis)
+        far_arr, new, field_out = (later, aux, sample.shape[along_dim])
+        leaves = tuple(((to_i, (to_i + 1) % far_arr) for to_i in range(far_arr)))
+        pieces_in = []
+        near = sample
+        for p in range(far_arr):
+            z2 = near if p == far_arr - 1 else lax.ppermute(near, axis_name=which_axis, perm=leaves)
+            frame_out = slab_in(near, (new - p) % far_arr * field_out)
+            pieces_in.append(frame_out)
+            near = z2
+        seen_now = jnp.stack(pieces_in, axis=0)
+        pieces_in = seen_now[(new - jnp.arange(far_arr)) % far_arr]
+        return point_scenes_in(pieces_in, array_axis)
+
+    partial_density = show_paths_in(
+        amplitude_triples,
+        "vir",
+        1,
+        lambda shard, offset: jnp.einsum("tae,tbe->ab", masked, shard, preferred_element_type=f32),
+        1,
     )
     density = lax.psum(partial_density, "occ")
     density = (density / jnp.sqrt(f32(triples_all * width))).astype(jnp.bfloat16)

time: 228 us -> 163 us (0.71)
  waiting for transfers between devices: 178 us -> 110 us
    all_gather x1, waiting for transfers between devices: 46.9 us -> 0.01 us  [on_device(): lax.all_gather(masked, 'vir', axis=1, tiled=True)]
    ppermute x0 -> x1, waiting for transfers between devices: none -> 37.9 us  [show_paths_in(): lax.ppermute(near, axis_name=which_axis, perm=leaves)]
    all_gather x1 -> x0, waiting for transfers between devices: 36.7 us -> none  [on_device(): lax.all_gather(amplitude_triples, 'vir', axis=1, tiled=True)]
    psum x1, waiting for transfers between devices: 93.5 us -> 71.9 us  [on_device(): density = lax.psum(partial_density, 'occ')]
    dot_general x1 -> x2, matrix products: 4.41 us -> 5.17 us  [on_device(): jnp.einsum('tae,tbe->ab', masked, shard, preferred_element_type=f32)]
  transfers between devices with their start and end apart: 3 -> 3, of which waited for: 3 -> 2; matrix products, arithmetic and copies ran while one was open for 8% -> 9% of each run, Pallas kernels for 0% -> 0%
where the time goes in v1:
time: 163 us; the launch traced here: 162 us
  waiting for transfers between devices  110 us (67%)
  matrix products  21 us (13%)
  between operations  14.9 us (9%)
  blocking collectives  10 us (6%)
  other arithmetic  2.55 us (2%)
  local copies, waits for them, and re-layouts  1.92 us (1%)
    psum x1, waiting for transfers between devices, on_device(): density = lax.psum(partial_density, 'occ')  71.9 us
    ppermute x1, waiting for transfers between devices, show_paths_in(): lax.ppermute(near, axis_name=which_axis, perm=leaves)  37.9 us
    dot_general x1, matrix products, on_device(): jnp.einsum('ac,tcb->tab', density, lax.all_gather(masked, 'vir', axis=1,...  6.99 us
    dot_general x1, matrix products, on_device(): jnp.einsum('tam,mb->tab', cycle_mid, doubles_full, preferred_element_type...  5.64 us
    all_gather x1, blocking collectives, on_device(): lax.all_gather(ladder_weight, 'vir', axis=1, tiled=True)  5.56 us
    dot_general x2, matrix products, on_device(): jnp.einsum('tae,tbe->ab', masked, shard, preferred_element_type=f32)  5.17 us
    all_gather x1, blocking collectives, on_device(): lax.all_gather(lambda_doubles, 'vir', axis=1, tiled=True)  4.46 us
  transfers between devices with their start and end apart: 3, of which 2 were waited for; matrix products, arithmetic and copies ran while one was open for 9% of the time, Pallas kernels for 0%

profile of v1, /device:TPU:8, one launch (start us, length us, event | category | flops | bytes accessed | tf_op | source)
XLA Modules:
  0.0 162.3 jit_solution(16166245806487901272)
XLA Ops:
  7.4 0.0 copy-start
  7.4 0.0 all-reduce.2.cloned.1.call-start
  7.4 1.5 collective-permute-start
  8.9 0.7 iota_compare_fusion
  9.6 1.8 %broadcast_select_fusion = bf16[16,160,320]{2,1,0:T(8,128)(2,1)S(1)} fusion(bf16[16,160,320]{2,1,0:T(8,128)(2,1)} %param.6, pred[16,320]{1,0:T(8,128)(4,1)S(1)} %iota_compare_fusion), kind=kLoop, calls=%fused_computation.3 | loop fusion | flops 819200 | bytes 3281920 | tf_op jit(solution)/shard_map/jit(_where)/select_n | solution.py:21
  11.4 0.0 copy-start.1
  11.4 2.9 %convolution_bitcast_fusion.1 = f32[1,160,160]{2,1,0:T(8,128)S(1)} fusion(bf16[16,160,320]{2,1,0:T(8,128)(2,1)S(1)} %broadcast_select_fusion, bf16[16,160,320]{2,1,0:T(8,128)(2,1)} %param.7), kind=kOutput, calls=%fused_computation.7 | convolution fusion | flops 262144000 | bytes 3379200 | tf_op jit(solution)/shard_map/tae,tbe->ab/dot_general | solution.py:52
  14.4 37.9 %collective-permute-done = bf16[16,160,320]{2,1,0:T(8,128)(2,1)} collective-permute-done((bf16[16,160,320]{2,1,0:T(8,128)(2,1)}, bf16[16,160,320]{2,1,0:T(8,128)(2,1)}, u32[]{:S(2)}, u32[]{:S(2)}) %collective-permute-start) | collective-permute-done | bytes 1638432 | tf_op jit(solution)/shard_map/ppermute | solution.py:40
  52.2 0.0 copy-done.1
  52.3 2.2 %convolution_bitcast_fusion = f32[1,160,160]{2,1,0:T(8,128)S(1)} fusion(bf16[16,160,320]{2,1,0:T(8,128)(2,1)S(1)} %broadcast_select_fusion, bf16[16,160,320]{2,1,0:T(8,128)(2,1)} %collective-permute-done), kind=kOutput, calls=%fused_computation.6 | convolution fusion | flops 262144000 | bytes 3379200 | tf_op jit(solution)/shard_map/tae,tbe->ab/dot_general | solution.py:52
  54.5 0.0 copy-start.4
  54.5 0.6 gather_fusion
  55.1 0.0 copy-start.3
  55.1 0.3 copy.11
  55.4 0.9 reshape.69
  56.3 0.0 all-reduce.2.cloned.1.call-update
  56.3 0.0 all-gather.3.cloned.1.call-start
  56.4 0.5 all-gather.3.cloned.1.call-update
  56.9 0.0 copy-done.4
  56.9 4.5 %all-gather = bf16[2,160,40]{1,2,0:T(8,128)(2,1)S(1)} all-gather(bf16[1,160,40]{1,2,0:T(8,128)(2,1)S(1)} %bitcast.37), channel_id=1, replica_groups=mesh['occ'=16,'vir'=2] {'vir'}, dimensions={0}, use_global_device_ids=true | all-gather | bytes 38400 | tf_op jit(solution)/shard_map/all_gather | solution.py:24
  61.4 0.1 reshape.82
  61.5 0.0 copy-done.3
  61.5 5.6 %all_gather.9 = bf16[320,320]{0,1:T(8,128)(2,1)S(1)} all-gather(bf16[320,160]{0,1:T(8,128)(2,1)S(1)} %copy-done.3), channel_id=1, replica_groups=mesh['occ'=16,'vir'=2] {'vir'}, dimensions={1}, use_global_device_ids=true | all-gather | bytes 307200 | tf_op jit(solution)/shard_map/all_gather | solution.py:23
  67.1 0.0 copy-done
  67.1 0.0 copy-start.2
  67.1 5.6 %fusion.1 = f32[16,160,320]{2,1,0:T(8,128)} fusion(bf16[320,40,1]{0,1,2:T(8,128)(2,1)S(1)} %reshape.82, bf16[16,160,320]{2,1,0:T(8,128)(2,1)} %param.7, bf16[320,40]{0,1:T(8,128)(2,1)S(1)} %copy-done), kind=kOutput, calls=%fused_computation.5 | convolution fusion | flops 131174400 | bytes 4966400 | tf_op jit(solution)/shard_map/tam,mb->tab/dot_general | solution.py:30
  72.7 0.0 copy-done.2
  72.7 3.2 %fusion.2 = f32[16,160,320]{2,1,0:T(8,128)} fusion(bf16[16,160,320]{2,1,0:T(8,128)(2,1)S(1)} %copy-done.2, bf16[320,320]{0,1:T(8,128)(2,1)S(1)} %all_gather.9), kind=kOutput, calls=%fused_computation.9 | convolution fusion | flops 524288000 | bytes 5120000 | tf_op jit(solution)/shard_map/tae,eb->tab/dot_general | solution.py:26
  76.0 71.9 %all-reduce.2.cloned.1.call-done = f32[160,320]{1,0:T(8,128)} async-done(((f32[160,320]{1,0:T(8,128)}), f32[160,320]{1,0:T(8,128)}) %all-reduce.2.cloned.1.call-update) | async-done | bytes 204816 | tf_op jit(solution)/shard_map/psum | solution.py:55
  147.9 0.0 all-gather.3.cloned.1.call-done
  147.9 7.0 %fusion = bf16[16,160,320]{2,1,0:T(8,128)(2,1)} fusion(f32[16,160,320]{2,1,0:T(8,128)} %fusion.2, f32[16,160,320]{2,1,0:T(8,128)} %fusion.1, bf16[16,320,320]{2,1,0:T(8,128)(2,1)} %all-gather.3.cloned.1.call-done, f32[160,320]{1,0:T(8,128)} %all-reduce.2.cloned.1.call-done), kind=kOutput, calls=%fused_computation.2 | convolution fusion | flops 527667200 | bytes 11673600 | tf_op jit(solution)/shard_map/ac,tcb->tab/dot_general | solution.py:57
  (4 shorter events, 0.1 us)
Async XLA Ops:
  7.4 59.7 %copy-start = (bf16[320,40]{0,1:T(8,128)(2,1)S(1)}, bf16[320,40]{0,1:T(8,128)(2,1)}, u32[]{:S(2)}) copy-start(bf16[320,40]{0,1:T(8,128)(2,1)} %param.10) | copy-start | bytes 76804
  7.4 140.5 %all-reduce.2.cloned.1.call-start = ((), (), s32[]{:S(2)}) async-start(), calls=%async_computation.1 | async-start | bytes 491520 | tf_op jit(solution)/shard_map/psum | solution.py:55
  7.4 44.9 %collective-permute-start = (bf16[16,160,320]{2,1,0:T(8,128)(2,1)}, bf16[16,160,320]{2,1,0:T(8,128)(2,1)}, u32[]{:S(2)}, u32[]{:S(2)}) collective-permute-start(bf16[16,160,320]{2,1,0:T(8,128)(2,1)} %param.7), channel_id=1, source_target_pairs={{0,1},{1,0},{2,3},{3,2},{4,5},{5,4},{6,7},{7,6},{8,9},{9,8},{10,11... | collective-permute-start | bytes 4915208 | tf_op jit(solution)/shard_map/ppermute | solution.py:40
  11.4 40.9 %copy-start.1 = (bf16[16,160,320]{2,1,0:T(8,128)(2,1)}, bf16[16,160,320]{2,1,0:T(8,128)(2,1)S(1)}, u32[]{:S(2)}) copy-start(bf16[16,160,320]{2,1,0:T(8,128)(2,1)S(1)} %broadcast_select_fusion) | copy-start | bytes 4915204
  54.5 2.4 %copy-start.4 = (bf16[40,160]{1,0:T(8,128)(2,1)S(1)}, bf16[40,160]{1,0:T(8,128)(2,1)}, u32[]{:S(2)}) copy-start(bf16[40,160]{1,0:T(8,128)(2,1)} %param.11) | copy-start | bytes 38404
  55.1 6.4 %copy-start.3 = (bf16[320,160]{0,1:T(8,128)(2,1)S(1)}, bf16[320,160]{0,1:T(8,128)(2,1)}, u32[]{:S(2)}) copy-start(bf16[320,160]{0,1:T(8,128)(2,1)} %param.9) | copy-start | bytes 307204
  56.3 91.5 %all-gather.3.cloned.1.call-start = ((), (), s32[]{:S(2)}) async-start(), calls=%async_computation | async-start | bytes 5898240 | tf_op jit(solution)/shard_map/all_gather | solution.py:60
  67.1 5.6 %copy-start.2 = (bf16[16,160,320]{2,1,0:T(8,128)(2,1)S(1)}, bf16[16,160,320]{2,1,0:T(8,128)(2,1)}, u32[]{:S(2)}) copy-start(bf16[16,160,320]{2,1,0:T(8,128)(2,1)} %copy-done.1) | copy-start | bytes 4915204
Sparse Core Ops, SparseCore 0:
  56.5 91.3 all-reduce.1
Sparse Core Ops, SparseCore 1:
  58.4 54.8 all-gather.2
